TPU v7x, 256 devices: a whole 4x4x8 slice. The times are simulated.
256 devices in a mesh: band: 8 (over x_lo, y), sector: 32 (over x_hi, z, core).
Axes of the slice: x: 4 (x_hi: 2, x_lo: 2; x = x_hi * 2 + x_lo), y: 4, z: 8, core: 2. Of those that a mesh axis runs over, the one named last changes fastest.
Arguments:
- grid_lat: bfloat16 [64, 2048, 512], P('band', 'sector'), may hold values from -6 to 6
- mesh_lat: bfloat16 [32768, 512], P(('band', 'sector')), may hold values from -6 to 6
- edge_feat: bfloat16 [393216, 512], P(('band', 'sector')), may hold values from -24 to 24
- edge_src: int32 [393216], P(('band', 'sector')), may hold values from 0 to 255, as said below
- edge_dst: int32 [393216], P(('band', 'sector')), may hold values from 0 to 511, as said below
- send_rows: int32 [32768], P(('band', 'sector')), may hold values from 0 to 127
- w_edge1: bfloat16 [1536, 512], replicated, may hold values from -0.15625 to 0.15625
- w_edge2: bfloat16 [512, 512], replicated, may hold values from -0.25 to 0.25
- edge_gain: float32 [512], replicated, may hold values from 0.25 to 1.75
- w_node1: bfloat16 [1024, 512], replicated, may hold values from -0.1875 to 0.1875
- w_node2: bfloat16 [512, 512], replicated, may hold values from -0.25 to 0.25
- node_gain: float32 [512], replicated, may hold values from 0.25 to 1.75
- cotangent: bfloat16 [64, 2048, 512], P('band', 'sector'), may hold values from -6 to 6
Outputs:
- grid_out: bfloat16 [64, 2048, 512], P('band', 'sector')
- grad_grid: bfloat16 [64, 2048, 512], P('band', 'sector')
- grad_mesh: bfloat16 [32768, 512], P(('band', 'sector'))
- grad_w_edge1: float32 [1536, 512], P('sector')
Inputs may be any that keep to these rules, and one draw needn't show every extreme that they name: `edge_src`: A device's mesh table is its 128 own rows followed by 32 rows each from the sector neighbour below, the sector neighbour above, the band neighbour below and the band neighbour above; devices of the first band never read the rows from below, those of the last band never the rows from above. `edge_dst`: each grid point of a device is the destination of exactly 3 of that device's edges; edges are in no particular order.
All inputs are finite; a program needn't handle non-finite values.
Results may differ from a plain program's by a relative error of at most 0.02.
Values may be sent and summed in bfloat16 or wider, within the bound.
No kernel may reach another device: no remote copies, remote signals or barrier semaphores. Data moves between devices by JAX's collectives and lax.ppermute only.
A program may use at most 64 MiB of HBM per device.

v0:
```python
import math
import jax
import jax.numpy as jnp
from jax import lax
from jax.sharding import PartitionSpec as P

EPSILON = 1e-05


def with_halo(shard, sides, width, wrap):
    for axis, dim in sides:
        devices, length = (lax.axis_size(axis), shard.shape[dim])
        up = [(i, (i + 1) % devices) for i in range(devices if wrap else devices - 1)]
        down = [(j, i) for i, j in up]
        last = lax.slice_in_dim(shard, length - width, length, axis=dim)
        initial = lax.slice_in_dim(shard, 0, width, axis=dim)
        before = lax.ppermute(last, axis, up)
        after = lax.ppermute(initial, axis, down)
        shard = jnp.concatenate([before, shard, after], axis=dim)
    return shard


def swish(values):
    return values * jax.nn.sigmoid(values)


def layer_norm(values, gain_vector):
    average = jnp.mean(values, axis=-1, keepdims=True)
    centred = values - average
    spread = jnp.mean(centred * centred, axis=-1, keepdims=True)
    return centred * lax.rsqrt(spread + EPSILON) * gain_vector


def decode_tail(pre_act, grid_wide, edge_dst, w_edge2, edge_gain, w_node1, w_node2, node_gain):
    hidden = swish(pre_act).astype(jnp.bfloat16)
    edge_raw = jnp.dot(hidden, w_edge2, preferred_element_type=jnp.float32)
    message = layer_norm(edge_raw, edge_gain).astype(jnp.bfloat16)
    points = grid_wide.shape[0]
    onehot = (edge_dst[None, :] == jnp.arange(points, dtype=jnp.int32)[:, None]).astype(
        jnp.bfloat16
    )
    aggregated = jnp.dot(onehot, message, preferred_element_type=jnp.float32).astype(jnp.bfloat16)
    node_input = jnp.concatenate([aggregated, grid_wide.astype(jnp.bfloat16)], axis=1)
    node_hidden = swish(jnp.dot(node_input, w_node1, preferred_element_type=jnp.float32)).astype(
        jnp.bfloat16
    )
    node_raw = jnp.dot(node_hidden, w_node2, preferred_element_type=jnp.float32)
    return (grid_wide + layer_norm(node_raw, node_gain)).astype(jnp.bfloat16)


def shards(
    grid_lat,
    mesh_lat,
    edge_feat,
    edge_src,
    edge_dst,
    send_rows,
    w_edge1,
    w_edge2,
    edge_gain,
    w_node1,
    w_node2,
    node_gain,
    cotangent,
):
    feature_width = w_edge2.shape[0]
    lat_rows = grid_lat.shape[0]
    lon_cols = grid_lat.shape[1]
    grid_block = grid_lat.reshape(lat_rows * lon_cols, feature_width)
    cot_block = cotangent.reshape(lat_rows * lon_cols, feature_width)
    own_rows = mesh_lat.shape[0]
    margin = send_rows.shape[0] // 4
    picked = jnp.take(mesh_lat, send_rows, axis=0)
    sector_recv = with_halo(picked[: 2 * margin], (("sector", 0),), margin, True)
    band_recv = with_halo(picked[2 * margin :], (("band", 0),), margin, False)
    mesh_table = jnp.concatenate(
        [
            mesh_lat,
            sector_recv[:margin],
            sector_recv[3 * margin :],
            band_recv[:margin],
            band_recv[3 * margin :],
        ],
        axis=0,
    )
    inputs = jnp.concatenate([edge_feat, mesh_table[edge_src], grid_block[edge_dst]], axis=1)
    pre_act = jnp.dot(inputs, w_edge1, preferred_element_type=jnp.float32)
    grid_wide = grid_block.astype(jnp.float32)

    def finish(pre_values, grid_values):
        return decode_tail(
            pre_values, grid_values, edge_dst, w_edge2, edge_gain, w_node1, w_node2, node_gain
        )

    result, pullback = jax.vjp(finish, pre_act, grid_wide)
    grad_pre, grad_tail = pullback(cot_block)
    grad_pre_b = grad_pre.astype(jnp.bfloat16)
    grad_inputs = lax.dot_general(
        grad_pre_b,
        w_edge1[feature_width:],
        (((1,), (1,)), ((), ())),
        preferred_element_type=jnp.float32,
    )
    grad_table = jax.ops.segment_sum(
        grad_inputs[:, :feature_width], edge_src, num_segments=mesh_table.shape[0]
    )
    grad_grid = grad_tail + jax.ops.segment_sum(
        grad_inputs[:, feature_width:], edge_dst, num_segments=grid_block.shape[0]
    )
    sector_back = with_halo(
        grad_table[own_rows : own_rows + 2 * margin].astype(jnp.bfloat16),
        (("sector", 0),),
        margin,
        True,
    ).astype(jnp.float32)
    band_back = with_halo(
        grad_table[own_rows + 2 * margin :].astype(jnp.bfloat16), (("band", 0),), margin, False
    ).astype(jnp.float32)
    returned = jnp.concatenate(
        [
            sector_back[:margin],
            sector_back[3 * margin :],
            band_back[:margin],
            band_back[3 * margin :],
        ],
        axis=0,
    )
    grad_mesh = (
        grad_table[:own_rows] + jax.ops.segment_sum(returned, send_rows, num_segments=own_rows)
    ).astype(jnp.bfloat16)
    total_edges = edge_feat.shape[0] * lax.axis_size("band") * lax.axis_size("sector")
    grad_scale = 1.0 / math.sqrt(total_edges)
    rows_out = 3 * feature_width // lax.axis_size("sector")
    full_grad = lax.dot_general(
        inputs, grad_pre_b, (((0,), (0,)), ((), ())), preferred_element_type=jnp.float32
    )
    summed = lax.psum(full_grad, ("band", "sector"))
    share_rows = lax.dynamic_slice_in_dim(summed, lax.axis_index("sector") * rows_out, rows_out, 0)
    grad_w_edge1 = share_rows * grad_scale
    grid_out = result.reshape(lat_rows, lon_cols, feature_width)
    grad_grid_out = grad_grid.astype(jnp.bfloat16).reshape(lat_rows, lon_cols, feature_width)
    return (grid_out, grad_grid_out, grad_mesh, grad_w_edge1)


def solution(mesh):
    in_specs = (
        P("band", "sector", None),
        P(("band", "sector"), None),
        P(("band", "sector"), None),
        P(("band", "sector")),
        P(("band", "sector")),
        P(("band", "sector")),
        P(),
        P(),
        P(),
        P(),
        P(),
        P(),
        P("band", "sector", None),
    )
    out_specs = (
        P("band", "sector", None),
        P("band", "sector", None),
        P(("band", "sector"), None),
        P("sector", None),
    )
    return jax.shard_map(shards, mesh=mesh, in_specs=in_specs, out_specs=out_specs, check_vma=False)
```

profile of v0, /device:TPU:2, one launch (start us, length us, event | category | flops | bytes accessed | tf_op | source)
XLA Modules:
  0.0 343.9 jit_solution(3824243465645055062)
XLA Ops:
  8.7 1.8 gather_fusion
  11.2 6.9 %collective-permute-start.1 = (bf16[32,512]{1,0:T(8,128)(2,1)}, bf16[32,512]{1,0:T(8,128)(2,1)S(1)}, u32[]{:S(2)}, u32[]{:S(2)}) collective-permute-start(bf16[32,512]{1,0:T(8,128)(2,1)} %get-tuple-element.21), channel_id=1, source_target_pairs={{1,0},{2,1},{3,2},{4,3},{5,4},{6,5},{7,6},{8,7},{9,8},{10,9},{11,1... | collective-permute-start | bytes 98312 | tf_op jit(solution)/shard_map/ppermute | solution.py:18
  18.1 3.5 %collective-permute-start.2 = (bf16[32,512]{1,0:T(8,128)(2,1)}, bf16[32,512]{1,0:T(8,128)(2,1)S(1)}, u32[]{:S(2)}, u32[]{:S(2)}) collective-permute-start(bf16[32,512]{1,0:T(8,128)(2,1)} %get-tuple-element.20), channel_id=1, source_target_pairs={{0,32},{32,64},{64,96},{96,128},{128,160},{160,192},{192,224},{1,3... | collective-permute-start | bytes 98312 | tf_op jit(solution)/shard_map/ppermute | solution.py:17
  21.6 4.5 %collective-permute-start.3 = (bf16[32,512]{1,0:T(8,128)(2,1)}, bf16[32,512]{1,0:T(8,128)(2,1)S(1)}, u32[]{:S(2)}, u32[]{:S(2)}) collective-permute-start(bf16[32,512]{1,0:T(8,128)(2,1)} %get-tuple-element.19), channel_id=1, source_target_pairs={{32,0},{64,32},{96,64},{128,96},{160,128},{192,160},{224,192},{33,... | collective-permute-start | bytes 98312 | tf_op jit(solution)/shard_map/ppermute | solution.py:18
  27.0 2.7 constant_dynamic-update-slice_fusion.7
  29.7 4.8 %gather_fusion.2 = bf16[1536,512]{1,0:T(8,128)(2,1)S(1)} fusion(bf16[512,512]{1,0:T(8,128)(2,1)S(1)} %bitcast.21, s32[2048]{0:T(1024)S(1)} %pad_clamp_fusion), kind=kCustom, calls=%fused_computation.2 | custom fusion | bytes 3151872 | tf_op jit(solution)/shard_map/gather | solution.py:86
  34.7 5.4 %gather_fusion.1 = bf16[1536,512]{1,0:T(8,128)(2,1)} fusion(bf16[256,512]{1,0:T(8,128)(2,1)S(1)} %constant_dynamic-update-slice_fusion, s32[2048]{0:T(1024)S(1)} %pad_clamp_fusion.1), kind=kCustom, calls=%fused_computation.1 | custom fusion | bytes 3151872 | tf_op jit(solution)/shard_map/gather | solution.py:86
  40.1 2.8 constant_dynamic-update-slice_fusion.6
  42.9 1.3 constant_dynamic-update-slice_fusion.5
  44.2 4.5 %fusion.69 = f32[1536,512]{1,0:T(8,128)S(1)} fusion(bf16[1536,1536]{1,0:T(8,128)(2,1)} %constant_dynamic-update-slice_fusion.5, bf16[1536,512]{1,0:T(8,128)(2,1)S(1)} %copy-done.10), kind=kOutput, calls=%fused_computation.121 | convolution fusion | flops 2415919104 | bytes 9437184 | tf_op jit(solution)/shard_map/dot_general | solution.py:87
  55.2 1.3 fusion.63
  56.5 3.6 %convolution_convert_fusion = bf16[512,1024]{1,0:T(8,128)(2,1)} fusion(bf16[1024,512]{1,0:T(8,128)(2,1)S(1)} %copy-done, f32[512,512]{1,0:T(8,128)} %copy-done.15, bf16[512,512]{1,0:T(8,128)(2,1)} %param.23, f32[512,512]{1,0:T(8,128)S(1)} %get-tuple-element.7, f32[512]{0:T(512)S(1)} %negate_multiply_fusion.1), kind=kOutput, calls=%fused_computation.39 | convolution fusion | flops 808976384 | bytes 4720640 | tf_op jit(solution)/shard_map/transpose(jvp())/dot_general | solution.py:44
  60.1 3.5 %multiply_reduce_fusion = (f32[1536]{0:T(1024)S(1)}, bf16[1536,512]{0,1:T(8,128)(2,1)S(1)}) fusion(f32[1536,512]{0,1:T(8,128)} %copy-done.2, f32[512]{0:T(512)S(1)} %copy-done.9, f32[1536]{0:T(1024)S(1)} %broadcast_multiply_fusion, bf16[512,1024]{1,0:T(8,128)(2,1)} %convolution_convert_fusion, s32[1536]{0:T(1024)S(1)} %copy-done.8), kind=kOutput, calls=%fused_computation.19 | convolution fusion | flops 810809856 | bytes 5263360 | tf_op jit(solution)/shard_map/transpose(jvp())/dot_general | solution.py:42
  65.7 2.6 fusion.1
  69.5 4.3 %fusion.70 = f32[1536,512]{1,0:T(8,128)} fusion(bf16[1536,1536]{1,0:T(8,128)(2,1)S(1)} %bitcast.26, bf16[1536,512]{1,0:T(8,128)(2,1)S(1)} %fusion.1), kind=kOutput, calls=%fused_computation.122 | convolution fusion | flops 2415919104 | bytes 9437184 | tf_op jit(solution)/shard_map/dot_general | solution.py:134
  73.8 6.2 %fusion.36 = f32[1536,1024]{1,0:T(8,128)} fusion(bf16[1536,512]{1,0:T(8,128)(2,1)} %copy-done.14, bf16[1536,512]{1,0:T(8,128)(2,1)} %param.19), kind=kOutput, calls=%fused_computation.55 | convolution fusion | flops 1610612736 | bytes 8912896 | tf_op jit(solution)/shard_map/dot_general | solution.py:98
  80.0 10.6 %scatter_custom_fusion.1 = f32[256,512]{1,0:T(8,128)S(1)} fusion(s32[1536]{0:T(1024)} %param.16, f32[1536,1024]{1,0:T(8,128)} %fusion.36, f32[]{:T(128)} %constant.22.clone.1), kind=kCustom, calls=%fused_computation.13 | custom fusion | flops 786432 | bytes 3670528 | tf_op jit(solution)/shard_map/scatter-add | solution.py:104
  90.6 3.7 %collective-permute-start.7 = (bf16[32,512]{1,0:T(8,128)(2,1)S(1)}, bf16[32,512]{1,0:T(8,128)(2,1)S(1)}, u32[]{:S(2)}, u32[]{:S(2)}) collective-permute-start(bf16[32,512]{1,0:T(8,128)(2,1)S(1)} %get-tuple-element.10), channel_id=1, source_target_pairs={{32,0},{64,32},{96,64},{128,96},{160,128},{192,160},{224,192},{33,... | collective-permute-start | bytes 98312 | tf_op jit(solution)/shard_map/ppermute | solution.py:18
  94.3 2.2 collective-permute-start.6
  97.7 10.9 %scatter_custom_fusion = f32[512,512]{1,0:T(8,128)S(1)} fusion(f32[512,512]{1,0:T(8,128)S(1)} %convert_add_fusion, s32[1536]{0:T(1024)S(1)} %copy-done.8, f32[1536,1024]{1,0:T(8,128)} %fusion.36), kind=kCustom, calls=%fused_computation.15 | custom fusion | flops 786432 | bytes 4194304 | tf_op jit(solution)/shard_map/scatter-add | solution.py:107
  111.1 5.4 %collective-permute-done.4 = bf16[32,512]{1,0:T(8,128)(2,1)S(1)} collective-permute-done((bf16[32,512]{1,0:T(8,128)(2,1)S(1)}, bf16[32,512]{1,0:T(8,128)(2,1)S(1)}, u32[]{:S(2)}, u32[]{:S(2)}) %collective-permute-start.4) | collective-permute-done | bytes 32800 | tf_op jit(solution)/shard_map/ppermute | solution.py:17
  116.5 1.6 scatter_custom_fusion.2
  118.8 216.7 %all-reduce.2.cloned.1.call-done = f32[1536,512]{1,0:T(8,128)} async-done(((f32[1536,512]{1,0:T(8,128)}), f32[1536,512]{1,0:T(8,128)}) %all-reduce.2.cloned.1.call-update) | async-done | bytes 3145744 | tf_op jit(solution)/shard_map/psum | solution.py:137
  335.5 1.5 dynamic-slice_multiply_fusion
  (90 shorter events, 17.2 us)
Async XLA Ops:
  7.2 45.1 %copy-start = (bf16[1024,512]{1,0:T(8,128)(2,1)S(1)}, bf16[1024,512]{1,0:T(8,128)(2,1)}, u32[]{:S(2)}) copy-start(bf16[1024,512]{1,0:T(8,128)(2,1)} %param.22) | copy-start | bytes 3145732
  7.2 22.5 %copy-start.6 = (s32[1536]{0:T(1024)S(1)}, s32[1536]{0:T(1024)}, u32[]{:S(2)}) copy-start(s32[1536]{0:T(1024)} %param.16) | copy-start | bytes 18436
  7.2 22.5 %copy-start.7 = (s32[1536]{0:T(1024)S(1)}, s32[1536]{0:T(1024)}, u32[]{:S(2)}) copy-start(s32[1536]{0:T(1024)} %param.17) | copy-start | bytes 18436
  7.2 22.5 %copy-start.1 = (bf16[8,64,512]{2,1,0:T(8,128)(2,1)S(1)}, bf16[8,64,512]{2,1,0:T(8,128)(2,1)}, u32[]{:S(2)}) copy-start(bf16[8,64,512]{2,1,0:T(8,128)(2,1)} %param.13) | copy-start | bytes 1572868
  7.2 328.3 %all-reduce.2.cloned.1.call-start = ((), (), s32[]{:S(2)}) async-start(), calls=%async_computation | async-start | bytes 6291456 | tf_op jit(solution)/shard_map/psum | solution.py:137
  11.2 23.3 %collective-permute-start = (bf16[32,512]{1,0:T(8,128)(2,1)}, bf16[32,512]{1,0:T(8,128)(2,1)S(1)}, u32[]{:S(2)}, u32[]{:S(2)}) collective-permute-start(bf16[32,512]{1,0:T(8,128)(2,1)} %get-tuple-element.22), channel_id=1, source_target_pairs={{0,1},{1,2},{2,3},{3,4},{4,5},{5,6},{6,7},{7,8},{8,9},{9,10},{10,1... | collective-permute-start | bytes 98312 | tf_op jit(solution)/shard_map/ppermute | solution.py:17
  11.2 23.3 %collective-permute-start.1 = (bf16[32,512]{1,0:T(8,128)(2,1)}, bf16[32,512]{1,0:T(8,128)(2,1)S(1)}, u32[]{:S(2)}, u32[]{:S(2)}) collective-permute-start(bf16[32,512]{1,0:T(8,128)(2,1)} %get-tuple-element.21), channel_id=1, source_target_pairs={{1,0},{2,1},{3,2},{4,3},{5,4},{6,5},{7,6},{8,7},{9,8},{10,9},{11,1... | collective-permute-start | bytes 98312 | tf_op jit(solution)/shard_map/ppermute | solution.py:18
  18.1 16.5 %collective-permute-start.2 = (bf16[32,512]{1,0:T(8,128)(2,1)}, bf16[32,512]{1,0:T(8,128)(2,1)S(1)}, u32[]{:S(2)}, u32[]{:S(2)}) collective-permute-start(bf16[32,512]{1,0:T(8,128)(2,1)} %get-tuple-element.20), channel_id=1, source_target_pairs={{0,32},{32,64},{64,96},{96,128},{128,160},{160,192},{192,224},{1,3... | collective-permute-start | bytes 98312 | tf_op jit(solution)/shard_map/ppermute | solution.py:17
  21.6 13.1 %collective-permute-start.3 = (bf16[32,512]{1,0:T(8,128)(2,1)}, bf16[32,512]{1,0:T(8,128)(2,1)S(1)}, u32[]{:S(2)}, u32[]{:S(2)}) collective-permute-start(bf16[32,512]{1,0:T(8,128)(2,1)} %get-tuple-element.19), channel_id=1, source_target_pairs={{32,0},{64,32},{96,64},{128,96},{160,128},{192,160},{224,192},{33,... | collective-permute-start | bytes 98312 | tf_op jit(solution)/shard_map/ppermute | solution.py:18
  40.1 4.1 %copy-start.10 = (bf16[1536,512]{1,0:T(8,128)(2,1)S(1)}, bf16[1536,512]{1,0:T(8,128)(2,1)}, u32[]{:S(2)}) copy-start(bf16[1536,512]{1,0:T(8,128)(2,1)} %param.19) | copy-start | bytes 4718596
  44.2 4.5 %copy-start.12 = (bf16[512,512]{1,0:T(8,128)(2,1)S(1)}, bf16[512,512]{1,0:T(8,128)(2,1)}, u32[]{:S(2)}) copy-start(bf16[512,512]{1,0:T(8,128)(2,1)} %param.20) | copy-start | bytes 1572868
  48.7 1.6 copy-start.16
  50.4 1.9 copy-start.2
  53.3 1.4 copy-start.4
  53.4 1.4 copy-start.5
  60.1 3.5 %copy-start.3 = (f32[1536,512]{0,1:T(8,128)S(1)}, f32[1536,512]{0,1:T(8,128)}, u32[]{:S(2)}) copy-start(f32[1536,512]{0,1:T(8,128)} %copy-done.2) | copy-start | bytes 9437188
  63.6 2.1 copy-start.17
  63.7 5.8 %slice-start = ((s8[4718592]{0:T(1024)(128)(4,1)}), s8[4194304]{0:T(1024)(128)(4,1)S(1)}, s32[]{:S(2)}) async-start(s8[4718592]{0:T(1024)(128)(4,1)} %bitcast.25), calls=%async_computation.1 | async-start | bytes 8388608
  65.7 3.8 %slice-start.1 = ((s8[4718592]{0:T(1024)(128)(4,1)}), s8[524288]{0:T(1024)(128)(4,1)S(1)}, s32[]{:S(2)}) async-start(s8[4718592]{0:T(1024)(128)(4,1)} %bitcast.25), calls=%async_computation.2 | async-start | bytes 1048576
  68.3 1.2 copy-start.14
  90.6 19.4 %collective-permute-start.7 = (bf16[32,512]{1,0:T(8,128)(2,1)S(1)}, bf16[32,512]{1,0:T(8,128)(2,1)S(1)}, u32[]{:S(2)}, u32[]{:S(2)}) collective-permute-start(bf16[32,512]{1,0:T(8,128)(2,1)S(1)} %get-tuple-element.10), channel_id=1, source_target_pairs={{32,0},{64,32},{96,64},{128,96},{160,128},{192,160},{224,192},{33,... | collective-permute-start | bytes 98312 | tf_op jit(solution)/shard_map/ppermute | solution.py:18
  94.3 15.7 %collective-permute-start.6 = (bf16[32,512]{1,0:T(8,128)(2,1)S(1)}, bf16[32,512]{1,0:T(8,128)(2,1)S(1)}, u32[]{:S(2)}, u32[]{:S(2)}) collective-permute-start(bf16[32,512]{1,0:T(8,128)(2,1)S(1)} %get-tuple-element.11), channel_id=1, source_target_pairs={{0,32},{32,64},{64,96},{96,128},{128,160},{160,192},{192,224},{1,3... | collective-permute-start | bytes 98312 | tf_op jit(solution)/shard_map/ppermute | solution.py:17
  109.5 1.6 collective-permute-start.5
  109.5 7.0 %collective-permute-start.4 = (bf16[32,512]{1,0:T(8,128)(2,1)S(1)}, bf16[32,512]{1,0:T(8,128)(2,1)S(1)}, u32[]{:S(2)}, u32[]{:S(2)}) collective-permute-start(bf16[32,512]{1,0:T(8,128)(2,1)S(1)} %get-tuple-element.9), channel_id=1, source_target_pairs={{0,1},{1,2},{2,3},{3,4},{4,5},{5,6},{6,7},{7,8},{8,9},{9,10},{10,1... | collective-permute-start | bytes 98312 | tf_op jit(solution)/shard_map/ppermute | solution.py:17
  (5 other events, 4.5 us)
Sparse Core Ops, SparseCore 0:
  73.9 261.5 all-reduce.1
where the time goes:
time: 344 us
  waiting for transfers between devices  223 us (65%)
  other arithmetic  32 us (9%)
  matrix products  28.2 us (8%)
  local copies, waits for them, and re-layouts  24.8 us (7%)
  starting transfers between devices  21.2 us (6%)
  between operations  14.5 us (4%)
    psum x1, waiting for transfers between devices, shards(): summed = lax.psum(full_grad, ('band', 'sector'))  217 us
    ppermute x4, starting transfers between devices, with_halo(): after = lax.ppermute(initial, axis, down)  15 us
    scatter-add x1, other arithmetic, shards(): jax.ops.segment_sum(grad_inputs[:, feature_width:], edge_dst, num_segment...  10.9 us
    unnamed x46, local copies, waits for them, and re-layouts  10.8 us
    scatter-add x1, other arithmetic, shards(): jax.ops.segment_sum(grad_inputs[:, :feature_width], edge_src, num_segment...  10.6 us
  transfers between devices with their start and end apart: 9, of which 3 were waited for; matrix products, arithmetic and copies ran while one was open for 12% of the time, Pallas kernels for 0%

commit v1 on v0

--- a/solution.py
+++ b/solution.py
@@ -134,7 +134,7 @@
     full_grad = lax.dot_general(
         inputs, grad_pre_b, (((0,), (0,)), ((), ())), preferred_element_type=jnp.float32
     )
-    summed = lax.psum(full_grad, ("band", "sector"))
+    summed = lax.psum(lax.psum(full_grad, "band"), "sector")
     share_rows = lax.dynamic_slice_in_dim(summed, lax.axis_index("sector") * rows_out, rows_out, 0)
     grad_w_edge1 = share_rows * grad_scale
     grid_out = result.reshape(lat_rows, lon_cols, feature_width)

time: 344 us -> 454 us (1.32)
  waiting for transfers between devices: 223 us -> 329 us
    psum x1 -> x2, waiting for transfers between devices: 217 us -> 322 us  [shards(): summed = lax.psum(lax.psum(full_grad, 'band'), 'sector')]
  transfers between devices with their start and end apart: 9 -> 10, of which waited for: 3 -> 4; matrix products, arithmetic and copies ran while one was open for 12% -> 9% of each run, Pallas kernels for 0% -> 0%
where the time goes in v1:
time: 454 us; the launch traced here: 451 us
  waiting for transfers between devices  329 us (72%)
  other arithmetic  32 us (7%)
  matrix products  28.2 us (6%)
  local copies, waits for them, and re-layouts  24.8 us (5%)
  starting transfers between devices  22.9 us (5%)
  between operations  14.5 us (3%)
    psum x2, waiting for transfers between devices, shards(): summed = lax.psum(lax.psum(full_grad, 'band'), 'sector')  322 us
    ppermute x4, starting transfers between devices, with_halo(): after = lax.ppermute(initial, axis, down)  17.4 us
    scatter-add x1, other arithmetic, shards(): jax.ops.segment_sum(grad_inputs[:, feature_width:], edge_dst, num_segment...  10.9 us
    unnamed x46, local copies, waits for them, and re-layouts  10.8 us
    scatter-add x1, other arithmetic, shards(): jax.ops.segment_sum(grad_inputs[:, :feature_width], edge_src, num_segment...  10.6 us
  transfers between devices with their start and end apart: 10, of which 4 were waited for; matrix products, arithmetic and copies ran while one was open for 9% of the time, Pallas kernels for 0%

profile of v1, /device:TPU:2, one launch (start us, length us, event | category | flops | bytes accessed | tf_op | source)
XLA Modules:
  0.0 451.2 jit_solution(15480822880825894098)
XLA Ops:
  8.7 1.8 gather_fusion
  11.2 6.9 %collective-permute-start.1 = (bf16[32,512]{1,0:T(8,128)(2,1)}, bf16[32,512]{1,0:T(8,128)(2,1)S(1)}, u32[]{:S(2)}, u32[]{:S(2)}) collective-permute-start(bf16[32,512]{1,0:T(8,128)(2,1)} %get-tuple-element.21), channel_id=1, source_target_pairs={{1,0},{2,1},{3,2},{4,3},{5,4},{6,5},{7,6},{8,7},{9,8},{10,9},{11,1... | collective-permute-start | bytes 98312 | tf_op jit(solution)/shard_map/ppermute | solution.py:18
  18.1 3.5 collective-permute-start.2
  21.6 4.5 collective-permute-start.3
  27.0 2.7 constant_dynamic-update-slice_fusion.7
  29.7 4.8 %gather_fusion.2 = bf16[1536,512]{1,0:T(8,128)(2,1)S(1)} fusion(bf16[512,512]{1,0:T(8,128)(2,1)S(1)} %bitcast.21, s32[2048]{0:T(1024)S(1)} %pad_clamp_fusion), kind=kCustom, calls=%fused_computation.2 | custom fusion | bytes 3151872 | tf_op jit(solution)/shard_map/gather | solution.py:86
  34.7 5.4 %gather_fusion.1 = bf16[1536,512]{1,0:T(8,128)(2,1)} fusion(bf16[256,512]{1,0:T(8,128)(2,1)S(1)} %constant_dynamic-update-slice_fusion, s32[2048]{0:T(1024)S(1)} %pad_clamp_fusion.1), kind=kCustom, calls=%fused_computation.1 | custom fusion | bytes 3151872 | tf_op jit(solution)/shard_map/gather | solution.py:86
  40.1 2.8 constant_dynamic-update-slice_fusion.6
  44.2 4.5 fusion.69
  56.5 3.6 convolution_convert_fusion
  60.1 3.5 multiply_reduce_fusion
  65.7 2.6 fusion.1
  69.5 4.3 fusion.70
  73.8 91.5 %all-reduce.3.cloned.1.call-done = f32[1536,512]{1,0:T(8,128)} async-done(((f32[1536,512]{1,0:T(8,128)}), f32[1536,512]{1,0:T(8,128)}) %all-reduce.3.cloned.1.call-update) | async-done | bytes 3145744 | tf_op jit(solution)/shard_map/psum | solution.py:137
  165.4 6.2 %fusion.36 = f32[1536,1024]{1,0:T(8,128)} fusion(bf16[1536,512]{1,0:T(8,128)(2,1)} %copy-done.14, bf16[1536,512]{1,0:T(8,128)(2,1)} %param.19), kind=kOutput, calls=%fused_computation.55 | convolution fusion | flops 1610612736 | bytes 8912896 | tf_op jit(solution)/shard_map/dot_general | solution.py:98
  171.6 10.6 %scatter_custom_fusion.1 = f32[256,512]{1,0:T(8,128)S(1)} fusion(s32[1536]{0:T(1024)} %param.16, f32[1536,1024]{1,0:T(8,128)} %fusion.36, f32[]{:T(128)} %constant.22.clone.1), kind=kCustom, calls=%fused_computation.13 | custom fusion | flops 786432 | bytes 3670528 | tf_op jit(solution)/shard_map/scatter-add | solution.py:104
  182.2 4.2 collective-permute-start.7
  186.5 1.9 collective-permute-start.6
  189.7 10.9 %scatter_custom_fusion = f32[512,512]{1,0:T(8,128)S(1)} fusion(f32[512,512]{1,0:T(8,128)S(1)} %convert_add_fusion, s32[1536]{0:T(1024)S(1)} %copy-done.8, f32[1536,1024]{1,0:T(8,128)} %fusion.36), kind=kCustom, calls=%fused_computation.15 | custom fusion | flops 786432 | bytes 4194304 | tf_op jit(solution)/shard_map/scatter-add | solution.py:107
  201.4 1.9 collective-permute-start.5
  203.3 1.6 collective-permute-done.5
  204.9 5.4 %collective-permute-done.4 = bf16[32,512]{1,0:T(8,128)(2,1)S(1)} collective-permute-done((bf16[32,512]{1,0:T(8,128)(2,1)S(1)}, bf16[32,512]{1,0:T(8,128)(2,1)S(1)}, u32[]{:S(2)}, u32[]{:S(2)}) %collective-permute-start.4) | collective-permute-done | bytes 32800 | tf_op jit(solution)/shard_map/ppermute | solution.py:17
  210.2 1.6 scatter_custom_fusion.2
  212.5 230.3 %all-reduce.5.cloned.1.call-done = f32[1536,512]{1,0:T(8,128)} async-done(((f32[1536,512]{1,0:T(8,128)}), f32[1536,512]{1,0:T(8,128)}) %all-reduce.5.cloned.1.call-update) | async-done | bytes 3145744 | tf_op jit(solution)/shard_map/psum | solution.py:137
  (93 shorter events, 19.9 us)
Async XLA Ops:
  7.2 45.1 %copy-start = (bf16[1024,512]{1,0:T(8,128)(2,1)S(1)}, bf16[1024,512]{1,0:T(8,128)(2,1)}, u32[]{:S(2)}) copy-start(bf16[1024,512]{1,0:T(8,128)(2,1)} %param.22) | copy-start | bytes 3145732
  7.2 22.5 %copy-start.6 = (s32[1536]{0:T(1024)S(1)}, s32[1536]{0:T(1024)}, u32[]{:S(2)}) copy-start(s32[1536]{0:T(1024)} %param.16) | copy-start | bytes 18436
  7.2 22.5 %copy-start.7 = (s32[1536]{0:T(1024)S(1)}, s32[1536]{0:T(1024)}, u32[]{:S(2)}) copy-start(s32[1536]{0:T(1024)} %param.17) | copy-start | bytes 18436
  7.2 22.5 %copy-start.1 = (bf16[8,64,512]{2,1,0:T(8,128)(2,1)S(1)}, bf16[8,64,512]{2,1,0:T(8,128)(2,1)}, u32[]{:S(2)}) copy-start(bf16[8,64,512]{2,1,0:T(8,128)(2,1)} %param.13) | copy-start | bytes 1572868
  7.2 158.2 %all-reduce.3.cloned.1.call-start = ((), (), s32[]{:S(2)}) async-start(), calls=%async_computation | async-start | bytes 6291456 | tf_op jit(solution)/shard_map/psum | solution.py:137
  11.2 23.3 %collective-permute-start = (bf16[32,512]{1,0:T(8,128)(2,1)}, bf16[32,512]{1,0:T(8,128)(2,1)S(1)}, u32[]{:S(2)}, u32[]{:S(2)}) collective-permute-start(bf16[32,512]{1,0:T(8,128)(2,1)} %get-tuple-element.22), channel_id=1, source_target_pairs={{0,1},{1,2},{2,3},{3,4},{4,5},{5,6},{6,7},{7,8},{8,9},{9,10},{10,1... | collective-permute-start | bytes 98312 | tf_op jit(solution)/shard_map/ppermute | solution.py:17
  11.2 23.3 %collective-permute-start.1 = (bf16[32,512]{1,0:T(8,128)(2,1)}, bf16[32,512]{1,0:T(8,128)(2,1)S(1)}, u32[]{:S(2)}, u32[]{:S(2)}) collective-permute-start(bf16[32,512]{1,0:T(8,128)(2,1)} %get-tuple-element.21), channel_id=1, source_target_pairs={{1,0},{2,1},{3,2},{4,3},{5,4},{6,5},{7,6},{8,7},{9,8},{10,9},{11,1... | collective-permute-start | bytes 98312 | tf_op jit(solution)/shard_map/ppermute | solution.py:18
  18.1 16.5 %collective-permute-start.2 = (bf16[32,512]{1,0:T(8,128)(2,1)}, bf16[32,512]{1,0:T(8,128)(2,1)S(1)}, u32[]{:S(2)}, u32[]{:S(2)}) collective-permute-start(bf16[32,512]{1,0:T(8,128)(2,1)} %get-tuple-element.20), channel_id=1, source_target_pairs={{0,32},{32,64},{64,96},{96,128},{128,160},{160,192},{192,224},{1,3... | collective-permute-start | bytes 98312 | tf_op jit(solution)/shard_map/ppermute | solution.py:17
  21.6 13.1 %collective-permute-start.3 = (bf16[32,512]{1,0:T(8,128)(2,1)}, bf16[32,512]{1,0:T(8,128)(2,1)S(1)}, u32[]{:S(2)}, u32[]{:S(2)}) collective-permute-start(bf16[32,512]{1,0:T(8,128)(2,1)} %get-tuple-element.19), channel_id=1, source_target_pairs={{32,0},{64,32},{96,64},{128,96},{160,128},{192,160},{224,192},{33,... | collective-permute-start | bytes 98312 | tf_op jit(solution)/shard_map/ppermute | solution.py:18
  40.1 4.1 copy-start.10
  44.2 4.5 copy-start.12
  48.7 1.6 copy-start.16
  50.4 1.9 copy-start.2
  53.3 1.4 copy-start.4
  53.4 1.4 copy-start.5
  60.1 3.5 copy-start.3
  63.6 2.1 copy-start.17
  63.7 5.8 %slice-start = ((s8[4718592]{0:T(1024)(128)(4,1)}), s8[4194304]{0:T(1024)(128)(4,1)S(1)}, s32[]{:S(2)}) async-start(s8[4718592]{0:T(1024)(128)(4,1)} %bitcast.25), calls=%async_computation.2 | async-start | bytes 8388608
  65.7 3.8 slice-start.1
  73.8 369.1 %all-reduce.5.cloned.1.call-start = ((), (), s32[]{:S(2)}) async-start(), calls=%async_computation.1 | async-start | bytes 6291456 | tf_op jit(solution)/shard_map/psum | solution.py:137
  182.2 21.0 %collective-permute-start.7 = (bf16[32,512]{1,0:T(8,128)(2,1)S(1)}, bf16[32,512]{1,0:T(8,128)(2,1)S(1)}, u32[]{:S(2)}, u32[]{:S(2)}) collective-permute-start(bf16[32,512]{1,0:T(8,128)(2,1)S(1)} %get-tuple-element.10), channel_id=1, source_target_pairs={{32,0},{64,32},{96,64},{128,96},{160,128},{192,160},{224,192},{33,... | collective-permute-start | bytes 98312 | tf_op jit(solution)/shard_map/ppermute | solution.py:18
  186.5 16.8 %collective-permute-start.6 = (bf16[32,512]{1,0:T(8,128)(2,1)S(1)}, bf16[32,512]{1,0:T(8,128)(2,1)S(1)}, u32[]{:S(2)}, u32[]{:S(2)}) collective-permute-start(bf16[32,512]{1,0:T(8,128)(2,1)S(1)} %get-tuple-element.11), channel_id=1, source_target_pairs={{0,32},{32,64},{64,96},{96,128},{128,160},{160,192},{192,224},{1,3... | collective-permute-start | bytes 98312 | tf_op jit(solution)/shard_map/ppermute | solution.py:17
  201.4 3.5 collective-permute-start.5
  203.3 7.0 %collective-permute-start.4 = (bf16[32,512]{1,0:T(8,128)(2,1)S(1)}, bf16[32,512]{1,0:T(8,128)(2,1)S(1)}, u32[]{:S(2)}, u32[]{:S(2)}) collective-permute-start(bf16[32,512]{1,0:T(8,128)(2,1)S(1)} %get-tuple-element.9), channel_id=1, source_target_pairs={{0,1},{1,2},{2,3},{3,4},{4,5},{5,6},{6,7},{7,8},{8,9},{9,10},{10,1... | collective-permute-start | bytes 98312 | tf_op jit(solution)/shard_map/ppermute | solution.py:17
  (6 other events, 5.7 us)
Sparse Core Ops, SparseCore 0:
  73.9 91.4 all-reduce.2
  168.0 274.7 all-reduce.4
